TPU v7x, 32 devices: a whole 2x2x4 slice. The times are simulated.
32 devices in a mesh: dp: 8 (over z, y), tensor: 4 (over x, core).
Axes of the slice: x: 2, y: 2, z: 4, core: 2. Of those that a mesh axis runs over, the one named last changes fastest.
Arguments:
- inputs: bfloat16 [8192, 1536], P('dp', 'tensor'), may hold values from -6 to 6
- segment_ids: int32 [8192], P('dp'), may hold values from 0 to 26, never falling along the last dimension, each value on 1 to 1000 neighbouring positions
- cotangent: bfloat16 [8192, 1536], P('dp', 'tensor'), may hold values from -6 to 6
- first_gain: bfloat16 [1536], replicated, may hold values from 0.5 to 1.5
- gate_weight: bfloat16 [1536, 2048], P(None, 'tensor'), may hold values from -0.15625 to 0.15625
- gate_bias: bfloat16 [2048], P('tensor'), may hold values from -3 to 3
- branch_weight: bfloat16 [1536, 2048], P(None, 'tensor'), may hold values from -0.15625 to 0.15625
- branch_bias: bfloat16 [2048], P('tensor'), may hold values from -3 to 3
- conv_weight: bfloat16 [4, 2048], P(None, 'tensor'), may hold values from -3 to 3
- conv_bias: bfloat16 [2048], P('tensor'), may hold values from -3 to 3
- rate_weight: bfloat16 [16, 128, 128], P('tensor'), may hold values from -0.5 to 0.5
- rate_bias: bfloat16 [2048], P('tensor'), may hold values from -3 to 3
- input_weight: bfloat16 [16, 128, 128], P('tensor'), may hold values from -0.5 to 0.5
- input_bias: bfloat16 [2048], P('tensor'), may hold values from -3 to 3
- decay_param: float32 [2048], P('tensor'), may hold values from 3 to 7
- out_weight: bfloat16 [2048, 1536], P('tensor'), may hold values from -0.25 to 0.25
- second_gain: bfloat16 [1536], replicated, may hold values from 0.5 to 1.5
- ffn_gate: bfloat16 [1536, 4608], P(None, 'tensor'), may hold values from -0.15625 to 0.15625
- ffn_up: bfloat16 [1536, 4608], P(None, 'tensor'), may hold values from -0.15625 to 0.15625
- ffn_down: bfloat16 [4608, 1536], P('tensor'), may hold values from -0.1875 to 0.1875
Outputs:
- output: bfloat16 [8192, 1536], P('dp', 'tensor')
- input_grad: float32 [8192, 1536], P('dp', 'tensor')
- first_gain_grad: float32 [1536], replicated
- gate_weight_grad: float32 [1536, 2048], P(None, 'tensor')
- gate_bias_grad: float32 [2048], P('tensor')
- branch_weight_grad: float32 [1536, 2048], P(None, 'tensor')
- branch_bias_grad: float32 [2048], P('tensor')
- conv_weight_grad: float32 [4, 2048], P(None, 'tensor')
- conv_bias_grad: float32 [2048], P('tensor')
- rate_weight_grad: float32 [16, 128, 128], P('tensor')
- rate_bias_grad: float32 [2048], P('tensor')
- input_weight_grad: float32 [16, 128, 128], P('tensor')
- input_bias_grad: float32 [2048], P('tensor')
- decay_grad: float32 [2048], P('tensor')
- out_weight_grad: float32 [2048, 1536], P('tensor')
- second_gain_grad: float32 [1536], replicated
- ffn_gate_grad: float32 [1536, 4608], P(None, 'tensor')
- ffn_up_grad: float32 [1536, 4608], P(None, 'tensor')
- ffn_down_grad: float32 [4608, 1536], P('tensor')
Inputs may be any that keep to these rules, and one draw needn't show every extreme that they name: `segment_ids`: segment numbers never fall along the tokens; each document has 1 to 1000 consecutive tokens, one exactly 1000.
All inputs are finite; a program needn't handle non-finite values.
Results may differ from a plain program's by a relative error of at most 0.013.
Values may be sent and summed in bfloat16 or wider, within the bound.
A program may use at most 256 MiB of HBM per device.

v0:
```python
import jax
import jax.numpy as jnp
from jax import lax
from jax.sharding import PartitionSpec as P

SEQ = 1024
EPSILON = 1e-06
FLOOR = 0.05


def rms_scale(values, gain):
    return values * lax.rsqrt(jnp.mean(values * values, axis=-1, keepdims=True) + EPSILON) * gain


def seq_masks(segments, length):
    count = segments.shape[0]
    place = jnp.arange(count, dtype=jnp.int32) % length
    previous = jnp.concatenate([segments[:1], segments[:-1]])
    reset = (place == 0) | (segments != previous)
    return (place, reset)


def conv_apply(values, weights, shift_bias, segments, place):
    total = shift_bias + weights[0] * values
    for offset in range(1, weights.shape[0]):
        moved = jnp.concatenate(
            [jnp.zeros((offset, values.shape[1]), values.dtype), values[:-offset]]
        )
        earlier = jnp.concatenate([jnp.full((offset,), -1, jnp.int32), segments[:-offset]])
        usable = ((place >= offset) & (segments == earlier)).astype(values.dtype)
        total = total + weights[offset] * moved * usable[:, None]
    return total


def gates_to_step(rate_pre, input_pre, conv_out, decay, reset):
    rate = jax.nn.sigmoid(rate_pre)
    opened = jax.nn.sigmoid(input_pre)
    decayed = jnp.exp(-8.0 * rate * jax.nn.softplus(-decay))
    keep = jnp.where(reset[:, None], jnp.zeros_like(decayed), decayed)
    scale = jnp.where(
        reset[:, None],
        jnp.ones_like(decayed),
        jnp.sqrt(jnp.maximum(1.0 - decayed * decayed, FLOOR)),
    )
    return (keep, scale * opened * conv_out)


def combine(earlier, later):
    return (earlier[0] * later[0], later[0] * earlier[1] + later[1])


def block_mix(values, weight):
    rows = values.shape[0]
    split = values.reshape(rows, weight.shape[0], -1)
    return jnp.einsum("thi,hij->thj", split, weight, preferred_element_type=jnp.float32).reshape(
        rows, -1
    )


def block_back(grads, weight):
    rows = grads.shape[0]
    split = grads.reshape(rows, weight.shape[0], -1)
    return jnp.einsum("thj,hij->thi", split, weight, preferred_element_type=jnp.float32).reshape(
        rows, -1
    )


def block_grad(values, grads, heads):
    rows = values.shape[0]
    left = values.reshape(rows, heads, -1)
    right = grads.reshape(rows, heads, -1)
    return jnp.einsum("thi,thj->hij", left, right, preferred_element_type=jnp.float32)


def column_sum(values):
    return jnp.sum(values.astype(jnp.float32), axis=0)


def body(
    inputs,
    segment_ids,
    cotangent,
    first_gain,
    gate_weight,
    gate_bias,
    branch_weight,
    branch_bias,
    conv_weight,
    conv_bias,
    rate_weight,
    rate_bias,
    input_weight,
    input_bias,
    decay_param,
    out_weight,
    second_gain,
    ffn_gate,
    ffn_up,
    ffn_down,
):
    share = inputs.shape[1]
    heads = rate_weight.shape[0]
    offset = lax.axis_index("tensor") * share
    place, reset = seq_masks(segment_ids, SEQ)
    whole_in = lax.all_gather(inputs, "tensor", axis=1, tiled=True).astype(jnp.float32)
    normed_one, first_pull = jax.vjp(rms_scale, whole_in, first_gain.astype(jnp.float32))
    normed_low = normed_one.astype(jnp.bfloat16)
    gate_pre = jnp.dot(
        normed_low, gate_weight, preferred_element_type=jnp.float32
    ) + gate_bias.astype(jnp.float32)
    branch_pre = jnp.dot(
        normed_low, branch_weight, preferred_element_type=jnp.float32
    ) + branch_bias.astype(jnp.float32)

    def conv_local(values, weights, shift_bias):
        return conv_apply(values, weights, shift_bias, segment_ids, place)

    conv_out, conv_pull = jax.vjp(
        conv_local, branch_pre, conv_weight.astype(jnp.float32), conv_bias.astype(jnp.float32)
    )
    conv_low = conv_out.astype(jnp.bfloat16)
    rate_pre = block_mix(conv_low, rate_weight) + rate_bias.astype(jnp.float32)
    input_pre = block_mix(conv_low, input_weight) + input_bias.astype(jnp.float32)

    def step_local(rate_in, input_in, driven, decay):
        return gates_to_step(rate_in, input_in, driven, decay, reset)

    (keep, drive), step_pull = jax.vjp(step_local, rate_pre, input_pre, conv_out, decay_param)
    state = lax.associative_scan(combine, (keep, drive))[1]
    gate_act, gelu_pull = jax.vjp(jax.nn.gelu, gate_pre)
    mixed_low = (gate_act * state).astype(jnp.bfloat16)
    partial_value = jnp.dot(mixed_low, out_weight, preferred_element_type=jnp.float32)
    resid = whole_in + lax.psum(partial_value, "tensor")
    resid_mine = lax.dynamic_slice_in_dim(resid, offset, share, 1)
    normed_two, second_pull = jax.vjp(rms_scale, resid, second_gain.astype(jnp.float32))
    two_low = normed_two.astype(jnp.bfloat16)
    hidden_gate = jnp.dot(two_low, ffn_gate, preferred_element_type=jnp.float32)
    hidden_up = jnp.dot(two_low, ffn_up, preferred_element_type=jnp.float32)
    hidden_act, hidden_pull = jax.vjp(jax.nn.gelu, hidden_gate)
    hidden_low = (hidden_act * hidden_up).astype(jnp.bfloat16)
    ffn_part = jnp.dot(hidden_low, ffn_down, preferred_element_type=jnp.float32)
    output = (
        resid_mine
        + lax.psum_scatter(
            ffn_part.astype(jnp.bfloat16), "tensor", scatter_dimension=1, tiled=True
        ).astype(jnp.float32)
    ).astype(jnp.bfloat16)
    whole_cot = lax.all_gather(cotangent, "tensor", axis=1, tiled=True)
    d_hidden = jnp.einsum("td,fd->tf", whole_cot, ffn_down, preferred_element_type=jnp.float32)
    ffn_down_grad = jnp.einsum(
        "tf,td->fd", hidden_low, whole_cot, preferred_element_type=jnp.float32
    )
    d_hgate = hidden_pull(d_hidden * hidden_up)[0].astype(jnp.bfloat16)
    d_hup = (d_hidden * hidden_act).astype(jnp.bfloat16)
    ffn_gate_grad = jnp.einsum("td,tf->df", two_low, d_hgate, preferred_element_type=jnp.float32)
    ffn_up_grad = jnp.einsum("td,tf->df", two_low, d_hup, preferred_element_type=jnp.float32)
    d_two_part = jnp.einsum(
        "tf,df->td", d_hgate, ffn_gate, preferred_element_type=jnp.float32
    ) + jnp.einsum("tf,df->td", d_hup, ffn_up, preferred_element_type=jnp.float32)
    d_two = lax.psum(d_two_part, "tensor")
    d_resid_norm, second_gain_grad = second_pull(d_two)
    d_resid = whole_cot.astype(jnp.float32) + d_resid_norm
    d_resid_low = d_resid.astype(jnp.bfloat16)
    out_weight_grad = jnp.einsum(
        "tr,td->rd", mixed_low, d_resid_low, preferred_element_type=jnp.float32
    )
    d_mixed = jnp.einsum("td,rd->tr", d_resid_low, out_weight, preferred_element_type=jnp.float32)
    d_gate_low = gelu_pull(d_mixed * state)[0].astype(jnp.bfloat16)
    d_state = d_mixed * gate_act
    channels = keep.shape[1]
    keep_next = jnp.concatenate([keep[1:], jnp.zeros((1, channels), jnp.float32)])
    adjoint = lax.associative_scan(combine, (keep_next, d_state), reverse=True)[1]
    state_prev = jnp.concatenate([jnp.zeros((1, channels), jnp.float32), state[:-1]])
    d_rate, d_input, d_conv_direct, decay_grad = step_pull((adjoint * state_prev, adjoint))
    d_rate_low = d_rate.astype(jnp.bfloat16)
    d_input_low = d_input.astype(jnp.bfloat16)
    rate_weight_grad = block_grad(conv_low, d_rate_low, heads)
    input_weight_grad = block_grad(conv_low, d_input_low, heads)
    rate_bias_grad = column_sum(d_rate_low)
    input_bias_grad = column_sum(d_input_low)
    d_conv = (
        d_conv_direct + block_back(d_rate_low, rate_weight) + block_back(d_input_low, input_weight)
    )
    d_branch, conv_weight_grad, conv_bias_grad = conv_pull(d_conv)
    d_branch_low = d_branch.astype(jnp.bfloat16)
    gate_weight_grad = jnp.einsum(
        "td,tr->dr", normed_low, d_gate_low, preferred_element_type=jnp.float32
    )
    branch_weight_grad = jnp.einsum(
        "td,tr->dr", normed_low, d_branch_low, preferred_element_type=jnp.float32
    )
    gate_bias_grad = column_sum(d_gate_low)
    branch_bias_grad = column_sum(d_branch_low)
    d_first_part = jnp.einsum(
        "tr,dr->td", d_gate_low, gate_weight, preferred_element_type=jnp.float32
    ) + jnp.einsum("tr,dr->td", d_branch_low, branch_weight, preferred_element_type=jnp.float32)
    d_first = lax.psum(d_first_part.astype(jnp.bfloat16), "tensor").astype(jnp.float32)
    d_in_norm, first_gain_grad = first_pull(d_first)
    input_grad = lax.dynamic_slice_in_dim(d_resid + d_in_norm, offset, share, 1)
    pieces = (
        lax.psum_scatter(first_gain_grad, "dp", scatter_dimension=0, tiled=True),
        lax.psum_scatter(gate_weight_grad, "dp", scatter_dimension=0, tiled=True),
        lax.psum_scatter(gate_bias_grad, "dp", scatter_dimension=0, tiled=True),
        lax.psum_scatter(branch_weight_grad, "dp", scatter_dimension=0, tiled=True),
        lax.psum_scatter(branch_bias_grad, "dp", scatter_dimension=0, tiled=True),
        lax.psum_scatter(conv_weight_grad, "dp", scatter_dimension=1, tiled=True),
        lax.psum_scatter(conv_bias_grad, "dp", scatter_dimension=0, tiled=True),
        lax.psum_scatter(rate_weight_grad, "dp", scatter_dimension=1, tiled=True),
        lax.psum_scatter(rate_bias_grad, "dp", scatter_dimension=0, tiled=True),
        lax.psum_scatter(input_weight_grad, "dp", scatter_dimension=1, tiled=True),
        lax.psum_scatter(input_bias_grad, "dp", scatter_dimension=0, tiled=True),
        lax.psum_scatter(decay_grad, "dp", scatter_dimension=0, tiled=True),
        lax.psum_scatter(out_weight_grad, "dp", scatter_dimension=0, tiled=True),
        lax.psum_scatter(second_gain_grad, "dp", scatter_dimension=0, tiled=True),
        lax.psum_scatter(ffn_gate_grad, "dp", scatter_dimension=0, tiled=True),
        lax.psum_scatter(ffn_up_grad, "dp", scatter_dimension=0, tiled=True),
        lax.psum_scatter(ffn_down_grad, "dp", scatter_dimension=1, tiled=True),
    )
    done = (
        lax.all_gather(pieces[0].astype(jnp.bfloat16), "dp", axis=0, tiled=True).astype(
            jnp.float32
        ),
        lax.all_gather(pieces[1].astype(jnp.bfloat16), "dp", axis=0, tiled=True).astype(
            jnp.float32
        ),
        lax.all_gather(pieces[2].astype(jnp.bfloat16), "dp", axis=0, tiled=True).astype(
            jnp.float32
        ),
        lax.all_gather(pieces[3].astype(jnp.bfloat16), "dp", axis=0, tiled=True).astype(
            jnp.float32
        ),
        lax.all_gather(pieces[4].astype(jnp.bfloat16), "dp", axis=0, tiled=True).astype(
            jnp.float32
        ),
        lax.all_gather(pieces[5].astype(jnp.bfloat16), "dp", axis=1, tiled=True).astype(
            jnp.float32
        ),
        lax.all_gather(pieces[6].astype(jnp.bfloat16), "dp", axis=0, tiled=True).astype(
            jnp.float32
        ),
        lax.all_gather(pieces[7].astype(jnp.bfloat16), "dp", axis=1, tiled=True).astype(
            jnp.float32
        ),
        lax.all_gather(pieces[8].astype(jnp.bfloat16), "dp", axis=0, tiled=True).astype(
            jnp.float32
        ),
        lax.all_gather(pieces[9].astype(jnp.bfloat16), "dp", axis=1, tiled=True).astype(
            jnp.float32
        ),
        lax.all_gather(pieces[10].astype(jnp.bfloat16), "dp", axis=0, tiled=True).astype(
            jnp.float32
        ),
        lax.all_gather(pieces[11].astype(jnp.bfloat16), "dp", axis=0, tiled=True).astype(
            jnp.float32
        ),
        lax.all_gather(pieces[12].astype(jnp.bfloat16), "dp", axis=0, tiled=True).astype(
            jnp.float32
        ),
        lax.all_gather(pieces[13].astype(jnp.bfloat16), "dp", axis=0, tiled=True).astype(
            jnp.float32
        ),
        lax.all_gather(pieces[14].astype(jnp.bfloat16), "dp", axis=0, tiled=True).astype(
            jnp.float32
        ),
        lax.all_gather(pieces[15].astype(jnp.bfloat16), "dp", axis=0, tiled=True).astype(
            jnp.float32
        ),
        lax.all_gather(pieces[16].astype(jnp.bfloat16), "dp", axis=1, tiled=True).astype(
            jnp.float32
        ),
    )
    return (
        output,
        input_grad,
        done[0],
        done[1],
        done[2],
        done[3],
        done[4],
        done[5],
        done[6],
        done[7],
        done[8],
        done[9],
        done[10],
        done[11],
        done[12],
        done[13],
        done[14],
        done[15],
        done[16],
    )


def solution(mesh):
    in_specs = (
        P("dp", "tensor"),
        P("dp"),
        P("dp", "tensor"),
        P(),
        P(None, "tensor"),
        P("tensor"),
        P(None, "tensor"),
        P("tensor"),
        P(None, "tensor"),
        P("tensor"),
        P("tensor", None, None),
        P("tensor"),
        P("tensor", None, None),
        P("tensor"),
        P("tensor"),
        P("tensor", None),
        P(),
        P(None, "tensor"),
        P(None, "tensor"),
        P("tensor", None),
    )
    out_specs = (
        P("dp", "tensor"),
        P("dp", "tensor"),
        P(),
        P(None, "tensor"),
        P("tensor"),
        P(None, "tensor"),
        P("tensor"),
        P(None, "tensor"),
        P("tensor"),
        P("tensor", None, None),
        P("tensor"),
        P("tensor", None, None),
        P("tensor"),
        P("tensor"),
        P("tensor", None),
        P(),
        P(None, "tensor"),
        P(None, "tensor"),
        P("tensor", None),
    )
    return jax.shard_map(body, mesh=mesh, in_specs=in_specs, out_specs=out_specs, check_vma=False)
```

profile of v0, /device:TPU:0, one launch (start us, length us, event | category | flops | bytes accessed | tf_op | source)
XLA Modules:
  0.0 2209.8 jit_solution(8797544625298831027)
XLA Ops:
  21.3 19.5 all-gather.10.cloned.1.call-done
  70.8 6.3 slice.535
  77.0 6.3 slice.536
  83.3 6.3 slice.534
  89.5 6.3 slice.538
  207.6 6.3 slice.533
  214.0 6.3 slice.606
  284.1 8.6 pad.169
  296.5 8.6 pad.168
  305.1 8.0 multiply_convert_fusion.4
  319.4 118.9 %all-reduce.76.cloned.1.call-done = f32[1024,1536]{1,0:T(8,128)} async-done(((f32[1024,1536]{1,0:T(8,128)}), f32[1024,1536]{1,0:T(8,128)}) %all-reduce.76.cloned.1.call-update) | async-done | bytes 6291472 | tf_op jit(solution)/shard_map/psum | solution.py:133
  447.3 5.8 fusion.119
  453.1 5.8 fusion.120
  458.9 9.7 all-gather.12.cloned.1.call-done
  468.6 12.3 multiply_convert_fusion.2
  485.2 6.2 convolution_add_fusion
  494.9 6.7 slice.611
  501.6 6.2 slice.618
  507.8 6.3 slice.609
  514.1 8.9 slice.612
  523.0 8.9 slice.619
  531.8 9.1 slice.610
  545.0 66.2 %all-reduce.78.cloned.1.call-done = f32[1024,1536]{1,0:T(8,128)} async-done(((f32[1024,1536]{1,0:T(8,128)}), f32[1024,1536]{1,0:T(8,128)}) %all-reduce.78.cloned.1.call-update) | async-done | bytes 6291472 | tf_op jit(solution)/shard_map/psum | solution.py:160
  611.2 6.3 multiply_reduce_fusion
  628.3 6.3 slice.613
  634.5 6.2 slice.615
  640.8 8.9 slice.614
  649.7 8.9 slice.616
  770.3 6.2 slice.687
  840.5 8.5 pad.189
  849.0 9.1 slice.688
  861.9 8.5 pad.188
  874.5 16.6 rev.2
  891.1 8.4 multiply_reduce_fusion.5
  913.1 6.7 multiply_reduce_fusion.9
  930.1 6.6 fusion.24
  936.8 5.9 fusion.86
  942.8 9.9 fusion.123
  952.8 10.0 fusion.124
  963.2 9.9 fusion.125
  980.9 6.1 fusion.122
  987.1 7.3 add_convert_fusion
  994.5 7.3 convolution_convert_fusion
  1008.3 73.4 %reduce-scatter.23.cloned.1.call-done = f32[64,1536]{1,0:T(8,128)} async-done(((f32[512,1536]{1,0:T(8,128)}), f32[64,1536]{1,0:T(8,128)}) %reduce-scatter.23.cloned.1.call-update) | async-done | bytes 393232 | tf_op jit(solution)/shard_map/reduce_scatter | solution.py:213
  1083.5 75.9 %reduce-scatter.15.cloned.1.call-done = f32[192,512]{1,0:T(8,128)} async-done(((f32[1536,512]{1,0:T(8,128)}), f32[192,512]{1,0:T(8,128)}) %reduce-scatter.15.cloned.1.call-update) | async-done | bytes 393232 | tf_op jit(solution)/shard_map/reduce_scatter | solution.py:202
  1161.3 130.8 %reduce-scatter.25.cloned.1.call-done = f32[192,1152]{1,0:T(8,128)} async-done(((f32[1536,1152]{1,0:T(8,128)}), f32[192,1152]{1,0:T(8,128)}) %reduce-scatter.25.cloned.1.call-update) | async-done | bytes 884752 | tf_op jit(solution)/shard_map/reduce_scatter | solution.py:215
  1294.1 130.5 %reduce-scatter.27.cloned.1.call-done = f32[192,1152]{1,0:T(8,128)} async-done(((f32[1536,1152]{1,0:T(8,128)}), f32[192,1152]{1,0:T(8,128)}) %reduce-scatter.27.cloned.1.call-update) | async-done | bytes 884752 | tf_op jit(solution)/shard_map/reduce_scatter | solution.py:216
  1426.7 130.4 %reduce-scatter.29.cloned.1.call-done = f32[1152,192]{0,1:T(8,128)} async-done(((f32[1152,1536]{0,1:T(8,128)}), f32[1152,192]{0,1:T(8,128)}) %reduce-scatter.29.cloned.1.call-update) | async-done | bytes 884752 | tf_op jit(solution)/shard_map/reduce_scatter | solution.py:217
  1567.7 54.5 %reduce-scatter.33.cloned.1.call-done = f32[64,4]{1,0:T(8,128)} async-done(((f32[512,4]{1,0:T(8,128)}), f32[64,4]{1,0:T(8,128)}) %reduce-scatter.33.cloned.1.call-update) | async-done | bytes 1040
  1623.0 18.6 all-gather
  1642.3 45.2 %reduce-scatter.19.cloned.1.call-done = f32[4,16,128]{2,1,0:T(8,128)} async-done(((f32[4,128,128]{2,1,0:T(8,128)}), f32[4,16,128]{2,1,0:T(8,128)}) %reduce-scatter.19.cloned.1.call-update) | async-done | bytes 32784 | tf_op jit(solution)/shard_map/reduce_scatter | solution.py:208
  1688.3 30.6 %all_gather.66 = bf16[4,128,128]{2,1,0:T(8,128)(2,1)S(1)} all-gather(bf16[4,16,128]{2,1,0:T(8,128)(2,1)S(1)} %convert_element_type.250), channel_id=1, replica_groups=mesh['dp'=8,'tensor'=4] {'dp'}, dimensions={1}, use_global_device_ids=true | all-gather | bytes 147456 | tf_op jit(solution)/shard_map/all_gather | solution.py:241
  1719.6 33.4 %reduce-scatter.21.cloned.1.call-done = f32[4,16,128]{2,1,0:T(8,128)} async-done(((f32[4,128,128]{2,1,0:T(8,128)}), f32[4,16,128]{2,1,0:T(8,128)}) %reduce-scatter.21.cloned.1.call-update) | async-done | bytes 32784 | tf_op jit(solution)/shard_map/reduce_scatter | solution.py:210
  1753.7 30.8 %all_gather.68 = bf16[4,128,128]{2,1,0:T(8,128)(2,1)S(1)} all-gather(bf16[4,16,128]{2,1,0:T(8,128)(2,1)S(1)} %convert_element_type.255), channel_id=1, replica_groups=mesh['dp'=8,'tensor'=4] {'dp'}, dimensions={1}, use_global_device_ids=true | all-gather | bytes 147456 | tf_op jit(solution)/shard_map/all_gather | solution.py:247
  1785.2 38.1 %all-reduce.80.cloned.1.call-done = bf16[1024,1536]{1,0:T(8,128)(2,1)} async-done(((bf16[1024,1536]{1,0:T(8,128)(2,1)}), bf16[1024,1536]{1,0:T(8,128)(2,1)}) %all-reduce.80.cloned.1.call-update) | async-done | bytes 3145744 | tf_op jit(solution)/shard_map/psum | solution.py:197
  1823.3 6.8 fusion
  1830.2 38.4 %all-reduce.70 = (bf16[1536]{0:T(1024)(128)(2,1)}, bf16[512]{0:T(512)(128)(2,1)}, bf16[512]{0:T(512)(128)(2,1)}, bf16[512]{0:T(512)(128)(2,1)}, bf16[512]{0:T(51...) all-reduce(f32[1536]{0:T(1024)} %get-tuple-element.116, ...), channel_id=3, replica_groups=mesh['dp'=8,'tensor'=4] {'dp'}, use_global_device_ids=true, to_apply=%region_9.10.clone | all-reduce | flops 6144 | bytes 36864
  1887.8 34.5 %all-reduce.71 = (bf16[1536]{0:T(1024)(128)(2,1)}, bf16[512]{0:T(512)(128)(2,1)}, bf16[512]{0:T(512)(128)(2,1)}, bf16[512]{0:T(512)(128)(2,1)}, bf16[512]{0:T(51...) all-reduce(bf16[1536]{0:T(1024)(128)(2,1)S(1)} %dynamic-update-slic, ...), channel_id=1, replica_groups=mesh['dp'=8,'tensor'=4] {'dp'}, use_global_device_ids=true, to_apply=%add.54 | all-reduce | flops 6144 | bytes 24576
  1945.6 10.5 all-gather.18.cloned.1.call-done
  1959.6 41.1 %all-gather.14.cloned.1.call-done = bf16[1536,512]{1,0:T(8,128)(2,1)} async-done(((bf16[192,512]{1,0:T(8,128)(2,1)}), bf16[1536,512]{1,0:T(8,128)(2,1)}) %all-gather.14.cloned.1.call-update) | async-done | bytes 1572880 | tf_op jit(solution)/shard_map/all_gather | solution.py:223
  2004.2 61.7 %all-gather.20.cloned.1.call-done = bf16[1536,1152]{1,0:T(8,128)(2,1)} async-done(((bf16[192,1152]{1,0:T(8,128)(2,1)}), bf16[1536,1152]{1,0:T(8,128)(2,1)}) %all-gather.20.cloned.1.call-update) | async-done | bytes 3538960 | tf_op jit(solution)/shard_map/all_gather | solution.py:262
  2071.3 60.0 %all-gather.22.cloned.1.call-done = bf16[1536,1152]{1,0:T(8,128)(2,1)} async-done(((bf16[192,1152]{1,0:T(8,128)(2,1)}), bf16[1536,1152]{1,0:T(8,128)(2,1)}) %all-gather.22.cloned.1.call-update) | async-done | bytes 3538960 | tf_op jit(solution)/shard_map/all_gather | solution.py:265
  2136.7 60.1 %all-gather.24.cloned.1.call-done = bf16[1152,1536]{0,1:T(8,128)(2,1)} async-done(((bf16[1152,192]{0,1:T(8,128)(2,1)}), bf16[1152,1536]{0,1:T(8,128)(2,1)}) %all-gather.24.cloned.1.call-update) | async-done | bytes 3538960 | tf_op jit(solution)/shard_map/all_gather | solution.py:268
  2196.8 6.0 copy.116
  (525 shorter events, 563.4 us)
Async XLA Ops:
  7.2 461.4 %copy-start = (bf16[1152,1536]{1,0:T(8,128)(2,1)S(1)}, bf16[1152,1536]{1,0:T(8,128)(2,1)}, u32[]{:S(2)}) copy-start(bf16[1152,1536]{1,0:T(8,128)(2,1)} %param.39) | copy-start | bytes 10616836
  7.2 33.6 %all-gather.10.cloned.1.call-start = ((), (), s32[]{:S(2)}) async-start(), calls=%async_computation.10 | async-start | bytes 3932160 | tf_op jit(solution)/shard_map/all_gather | solution.py:105
  7.9 430.4 %all-reduce.76.cloned.1.call-start = ((), (), s32[]{:S(2)}) async-start(), calls=%async_computation.11 | async-start | bytes 12582912 | tf_op jit(solution)/shard_map/psum | solution.py:133
  13.9 51.3 %copy-start.15 = (f32[512]{0:T(512)}, f32[512]{0:T(512)S(1)}, u32[]{:S(2)}) copy-start(f32[512]{0:T(512)S(1)} %convert_element_type.215) | copy-start | bytes 6148
  21.3 26.2 %copy-start.17 = (f32[1024]{0:T(1024)}, f32[1024]{0:T(1024)S(1)}, u32[]{:S(2)}) copy-start(f32[1024]{0:T(1024)S(1)} %get-tuple-element.209) | copy-start | bytes 12292
  21.3 26.2 %copy-start.19 = (f32[1024]{0:T(1024)}, f32[1024]{0:T(1024)S(1)}, u32[]{:S(2)}) copy-start(f32[1024]{0:T(1024)S(1)} %get-tuple-element.214) | copy-start | bytes 12292
  21.3 26.2 %copy-start.21 = (f32[1024]{0:T(1024)}, f32[1024]{0:T(1024)S(1)}, u32[]{:S(2)}) copy-start(f32[1024]{0:T(1024)S(1)} %get-tuple-element.215) | copy-start | bytes 12292
  207.6 14.0 copy-start.45
  207.6 14.0 copy-start.59
  234.8 18.4 copy-start.55
  253.2 11.0 copy-start.53
  296.5 8.6 copy-start.24
  296.5 8.6 copy-start.31
  296.5 8.6 copy-start.64
  305.1 9.0 copy-start.74
  318.6 150.0 %all-gather.12.cloned.1.call-start = ((), (), s32[]{:S(2)}) async-start(), calls=%async_computation.12 | async-start | bytes 3932160 | tf_op jit(solution)/shard_map/all_gather | solution.py:148
  319.3 291.9 %all-reduce.78.cloned.1.call-start = ((), (), s32[]{:S(2)}) async-start(), calls=%async_computation.13 | async-start | bytes 12582912 | tf_op jit(solution)/shard_map/psum | solution.py:160
  442.9 4.4 copy-start.70
  447.3 5.8 copy-start.12
  447.3 5.8 copy-start.72
  468.6 12.3 copy-start.71
  480.9 4.3 copy-start.79
  480.9 4.3 copy-start.78
  480.9 4.3 copy-start.73
  491.5 515.1 %reduce-scatter.17.cloned.1.call-start = ((), (), s32[]{:S(2)}) async-start(), calls=%async_computation.17 | async-start | bytes 3538944 | tf_op jit(solution)/shard_map/reduce_scatter | solution.py:204
  611.2 6.4 copy-start.8
  611.2 7.4 copy-start.11
  618.6 4.6 copy-start.77
  622.5 5.8 copy-start.7
  761.6 16.2 copy-start.46
  761.6 16.3 copy-start.60
  791.0 18.4 copy-start.56
  809.5 11.0 copy-start.54
  874.5 16.6 copy-start.16
  874.5 16.6 copy-start.34
  874.5 16.6 copy-start.36
  874.5 16.6 copy-start.48
  891.1 8.4 copy-start.61
  891.1 9.0 copy-start.4
  913.1 6.8 copy-start.2
  913.1 6.8 copy-start.18
  913.1 6.7 copy-start.20
  929.9 151.9 %reduce-scatter.23.cloned.1.call-start = ((), (), s32[]{:S(2)}) async-start(), calls=%async_computation.21 | async-start | bytes 3538944 | tf_op jit(solution)/shard_map/reduce_scatter | solution.py:213
  936.7 222.8 %reduce-scatter.15.cloned.1.call-start = ((), (), s32[]{:S(2)}) async-start(), calls=%async_computation.15 | async-start | bytes 3538944 | tf_op jit(solution)/shard_map/reduce_scatter | solution.py:202
  942.7 349.3 %reduce-scatter.25.cloned.1.call-start = ((), (), s32[]{:S(2)}) async-start(), calls=%async_computation.23 | async-start | bytes 7962624 | tf_op jit(solution)/shard_map/reduce_scatter | solution.py:215
  952.7 471.9 %reduce-scatter.27.cloned.1.call-start = ((), (), s32[]{:S(2)}) async-start(), calls=%async_computation.25 | async-start | bytes 7962624 | tf_op jit(solution)/shard_map/reduce_scatter | solution.py:216
  962.8 594.3 %reduce-scatter.29.cloned.1.call-start = ((), (), s32[]{:S(2)}) async-start(), calls=%async_computation.27 | async-start | bytes 7962624 | tf_op jit(solution)/shard_map/reduce_scatter | solution.py:217
  973.2 649.0 %reduce-scatter.33.cloned.1.call-start = ((), (), s32[]{:S(2)}) async-start(), calls=%async_computation.30 | async-start | bytes 294912
  975.4 712.1 %reduce-scatter.19.cloned.1.call-start = ((), (), s32[]{:S(2)}) async-start(), calls=%async_computation.19 | async-start | bytes 294912 | tf_op jit(solution)/shard_map/reduce_scatter | solution.py:208
  978.2 774.8 %reduce-scatter.21.cloned.1.call-start = ((), (), s32[]{:S(2)}) async-start(), calls=%async_computation.20 | async-start | bytes 294912 | tf_op jit(solution)/shard_map/reduce_scatter | solution.py:210
  987.1 836.3 %all-reduce.80.cloned.1.call-start = ((), (), s32[]{:S(2)}) async-start(), calls=%async_computation.14 | async-start | bytes 6291456 | tf_op jit(solution)/shard_map/psum | solution.py:197
  994.5 942.5 %reduce-scatter.31.cloned.1.call-start = ((), (), s32[]{:S(2)}) async-start(), calls=%async_computation.29 | async-start | bytes 3932160
  1006.5 935.6 %all-gather.16.cloned.1.call-start = ((), (), s32[]{:S(2)}) async-start(), calls=%async_computation.18 | async-start | bytes 1769472 | tf_op jit(solution)/shard_map/all_gather | solution.py:229
  1008.3 947.8 %all-gather.18.cloned.1.call-start = ((), (), s32[]{:S(2)}) async-start(), calls=%async_computation.22 | async-start | bytes 1769472 | tf_op jit(solution)/shard_map/all_gather | solution.py:256
  1083.5 917.2 %all-gather.14.cloned.1.call-start = ((), (), s32[]{:S(2)}) async-start(), calls=%async_computation.16 | async-start | bytes 1769472 | tf_op jit(solution)/shard_map/all_gather | solution.py:223
  1161.2 904.7 %all-gather.20.cloned.1.call-start = ((), (), s32[]{:S(2)}) async-start(), calls=%async_computation.24 | async-start | bytes 3981312 | tf_op jit(solution)/shard_map/all_gather | solution.py:262
  1294.1 265.0 %copy-start.63 = (u32[32]{0:T(128)S(1)}, u32[32]{0:T(128)}, u32[]{:S(2)}) copy-start(u32[32]{0:T(128)} %constant.193) | copy-start | bytes 388
  1294.1 837.2 %all-gather.22.cloned.1.call-start = ((), (), s32[]{:S(2)}) async-start(), calls=%async_computation.26 | async-start | bytes 3981312 | tf_op jit(solution)/shard_map/all_gather | solution.py:265
  1426.6 770.2 %all-gather.24.cloned.1.call-start = ((), (), s32[]{:S(2)}) async-start(), calls=%async_computation.28 | async-start | bytes 3981312 | tf_op jit(solution)/shard_map/all_gather | solution.py:268
  1785.2 45.0 %copy-start.29 = (f32[1536]{0:T(1024)S(1)}, f32[1536]{0:T(1024)}, u32[]{:S(2)}) copy-start(f32[1536]{0:T(1024)} %get-tuple-element.114) | copy-start | bytes 18436
  1785.2 147.2 %copy-start.28 = (f32[1024]{0:T(1024)S(1)}, f32[1024]{0:T(1024)}, u32[]{:S(2)}) copy-start(f32[1024]{0:T(1024)} %copy-done.27) | copy-start | bytes 12292
  1785.2 147.9 %copy-start.26 = (f32[1024]{0:T(1024)S(1)}, f32[1024]{0:T(1024)}, u32[]{:S(2)}) copy-start(f32[1024]{0:T(1024)} %copy-done.23) | copy-start | bytes 12292
  1878.2 5.2 copy-start.68
  1879.0 6.6 copy-start.69
  (37 other events, 93.8 us)
Sparse Core Ops, SparseCore 0:
  9.6 31.1 all-gather.9
  318.7 119.5 all-reduce.75
  439.9 28.6 all-gather.11
  491.6 119.5 all-reduce.77
  930.0 74.7 reduce-scatter.16
  1008.2 73.4 reduce-scatter.22
  1085.3 74.0 reduce-scatter.14
  1163.7 128.2 reduce-scatter.24
  1296.3 128.2 reduce-scatter.26
  1428.7 128.2 reduce-scatter.28
  1560.9 61.1 reduce-scatter.32
  1625.9 61.5 reduce-scatter.18
  1691.4 61.5 reduce-scatter.20
  1755.8 67.5 all-reduce.79
  1826.3 37.9 reduce-scatter.30
  1866.9 44.3 all-gather.15
  1913.4 42.6 all-gather.17
  1958.1 42.5 all-gather.13
  2002.9 62.9 all-gather.19
  2067.9 63.3 all-gather.21
  2133.5 63.3 all-gather.23
where the time goes:
time: 2230 us; the launch traced here: 2210 us
  waiting for transfers between devices  1160 us (52%)
  local copies, waits for them, and re-layouts  501 us (22%)
  other arithmetic  237 us (11%)
  blocking collectives  153 us (7%)
  matrix products  138 us (6%)
    slice x66, local copies, waits for them, and re-layouts, body(): lax.associative_scan(combine, (keep_next, d_state), reverse=True)[1]  185 us
    slice x60, local copies, waits for them, and re-layouts, body(): state = lax.associative_scan(combine, (keep, drive))[1]  131 us
    reduce_scatter x1, waiting for transfers between devices, body(): lax.psum_scatter(ffn_gate_grad, 'dp', scatter_dimension=0, tiled=True)  131 us
    reduce_scatter x1, waiting for transfers between devices, body(): lax.psum_scatter(ffn_up_grad, 'dp', scatter_dimension=0, tiled=True)  130 us
    reduce_scatter x1, waiting for transfers between devices, body(): lax.psum_scatter(ffn_down_grad, 'dp', scatter_dimension=1, tiled=True)  130 us
    psum x1, waiting for transfers between devices, body(): resid = whole_in + lax.psum(partial_value, 'tensor')  119 us
    reduce_scatter x1, waiting for transfers between devices, body(): lax.psum_scatter(gate_weight_grad, 'dp', scatter_dimension=0, tiled=True)  75.9 us
    reduce_scatter x1, waiting for transfers between devices, body(): lax.psum_scatter(out_weight_grad, 'dp', scatter_dimension=0, tiled=True)  73.4 us
  transfers between devices with their start and end apart: 21, of which 18 were waited for; matrix products, arithmetic and copies ran while one was open for 11% of the time, Pallas kernels for 0%

commit v1 on v0

--- a/solution.py
+++ b/solution.py
@@ -130,7 +130,7 @@
     gate_act, gelu_pull = jax.vjp(jax.nn.gelu, gate_pre)
     mixed_low = (gate_act * state).astype(jnp.bfloat16)
     partial_value = jnp.dot(mixed_low, out_weight, preferred_element_type=jnp.float32)
-    resid = whole_in + lax.psum(partial_value, "tensor")
+    resid = whole_in + jnp.sum(lax.all_gather(partial_value, "tensor"), axis=0)
     resid_mine = lax.dynamic_slice_in_dim(resid, offset, share, 1)
     normed_two, second_pull = jax.vjp(rms_scale, resid, second_gain.astype(jnp.float32))
     two_low = normed_two.astype(jnp.bfloat16)

time: 2230 us -> 2270 us (1.018)
  waiting for transfers between devices: 1160 us -> 1190 us
    all_gather x0 -> x1, waiting for transfers between devices: none -> 154 us  [body(): resid = whole_in + jnp.sum(lax.all_gather(partial_value, 'tensor'), axis=0)]
    psum x1 -> x0, waiting for transfers between devices: 119 us -> none  [body(): resid = whole_in + lax.psum(partial_value, 'tensor')]
  transfers between devices with their start and end apart: 21 -> 21, of which waited for: 18 -> 17; matrix products, arithmetic and copies ran while one was open for 11% -> 12% of each run, Pallas kernels for 0% -> 0%
where the time goes in v1:
time: 2270 us; the launch traced here: 2250 us
  waiting for transfers between devices  1190 us (52%)
  local copies, waits for them, and re-layouts  501 us (22%)
  other arithmetic  250 us (11%)
  blocking collectives  153 us (7%)
  matrix products  138 us (6%)
    slice x66, local copies, waits for them, and re-layouts, body(): lax.associative_scan(combine, (keep_next, d_state), reverse=True)[1]  185 us
    all_gather x1, waiting for transfers between devices, body(): resid = whole_in + jnp.sum(lax.all_gather(partial_value, 'tensor'), axis=0)  154 us
    slice x60, local copies, waits for them, and re-layouts, body(): state = lax.associative_scan(combine, (keep, drive))[1]  131 us
    reduce_scatter x1, waiting for transfers between devices, body(): lax.psum_scatter(ffn_gate_grad, 'dp', scatter_dimension=0, tiled=True)  131 us
    reduce_scatter x1, waiting for transfers between devices, body(): lax.psum_scatter(ffn_up_grad, 'dp', scatter_dimension=0, tiled=True)  130 us
    reduce_scatter x1, waiting for transfers between devices, body(): lax.psum_scatter(ffn_down_grad, 'dp', scatter_dimension=1, tiled=True)  130 us
    reduce_scatter x1, waiting for transfers between devices, body(): lax.psum_scatter(gate_weight_grad, 'dp', scatter_dimension=0, tiled=True)  75.4 us
    reduce_scatter x1, waiting for transfers between devices, body(): lax.psum_scatter(out_weight_grad, 'dp', scatter_dimension=0, tiled=True)  73.4 us
  transfers between devices with their start and end apart: 21, of which 17 were waited for; matrix products, arithmetic and copies ran while one was open for 12% of the time, Pallas kernels for 0%

profile of v1, /device:TPU:0, one launch (start us, length us, event | category | flops | bytes accessed | tf_op | source)
XLA Modules:
  0.0 2248.2 jit_solution(16707874555614285354)
XLA Ops:
  21.2 19.6 all-gather.12.cloned.1.call-done
  70.8 6.3 slice.535
  77.0 6.3 slice.536
  83.3 6.3 slice.534
  89.6 6.3 slice.538
  207.7 6.3 slice.533
  214.0 6.3 slice.606
  284.1 8.6 pad.169
  296.5 8.6 pad.168
  305.1 8.1 multiply_convert_fusion.4
  319.4 154.1 %all-gather.28.cloned.1.call-done = f32[4096,1536]{1,0:T(8,128)} async-done(((f32[1024,1536]{1,0:T(8,128)}), f32[4096,1536]{1,0:T(8,128)}) %all-gather.28.cloned.1.call-update) | async-done | bytes 25165840 | tf_op jit(solution)/shard_map/all_gather | solution.py:133
  473.6 13.6 reduce_sum.149
  496.2 5.8 fusion.119
  502.0 5.8 fusion.120
  507.8 12.3 multiply_convert_fusion.2
  524.4 6.2 convolution_add_fusion
  534.0 6.7 slice.611
  540.7 6.2 slice.618
  547.0 6.3 slice.609
  553.2 8.9 slice.612
  562.1 8.9 slice.619
  571.0 9.2 slice.610
  584.3 66.0 %all-reduce.75.cloned.1.call-done = f32[1024,1536]{1,0:T(8,128)} async-done(((f32[1024,1536]{1,0:T(8,128)}), f32[1024,1536]{1,0:T(8,128)}) %all-reduce.75.cloned.1.call-update) | async-done | bytes 6291472 | tf_op jit(solution)/shard_map/psum | solution.py:160
  650.3 6.3 multiply_reduce_fusion
  667.4 6.2 slice.613
  673.6 6.2 slice.615
  679.8 8.9 slice.614
  688.7 8.9 slice.616
  809.3 6.2 slice.687
  879.4 8.5 pad.189
  887.9 9.1 slice.688
  900.7 8.5 pad.188
  913.3 16.6 rev.2
  929.9 8.4 multiply_reduce_fusion.5
  951.9 6.7 multiply_reduce_fusion.9
  968.9 6.7 fusion.24
  975.7 5.9 fusion.86
  981.6 9.9 fusion.123
  991.6 10.0 fusion.124
  1002.1 9.9 fusion.125
  1019.8 6.1 fusion.122
  1026.0 7.3 add_convert_fusion
  1033.4 7.3 convolution_convert_fusion
  1047.2 73.4 %reduce-scatter.23.cloned.1.call-done = f32[64,1536]{1,0:T(8,128)} async-done(((f32[512,1536]{1,0:T(8,128)}), f32[64,1536]{1,0:T(8,128)}) %reduce-scatter.23.cloned.1.call-update) | async-done | bytes 393232 | tf_op jit(solution)/shard_map/reduce_scatter | solution.py:213
  1122.3 75.4 %reduce-scatter.15.cloned.1.call-done = f32[192,512]{1,0:T(8,128)} async-done(((f32[1536,512]{1,0:T(8,128)}), f32[192,512]{1,0:T(8,128)}) %reduce-scatter.15.cloned.1.call-update) | async-done | bytes 393232 | tf_op jit(solution)/shard_map/reduce_scatter | solution.py:202
  1199.5 130.7 %reduce-scatter.25.cloned.1.call-done = f32[192,1152]{1,0:T(8,128)} async-done(((f32[1536,1152]{1,0:T(8,128)}), f32[192,1152]{1,0:T(8,128)}) %reduce-scatter.25.cloned.1.call-update) | async-done | bytes 884752 | tf_op jit(solution)/shard_map/reduce_scatter | solution.py:215
  1332.4 130.5 %reduce-scatter.27.cloned.1.call-done = f32[192,1152]{1,0:T(8,128)} async-done(((f32[1536,1152]{1,0:T(8,128)}), f32[192,1152]{1,0:T(8,128)}) %reduce-scatter.27.cloned.1.call-update) | async-done | bytes 884752 | tf_op jit(solution)/shard_map/reduce_scatter | solution.py:216
  1464.9 130.3 %reduce-scatter.29.cloned.1.call-done = f32[1152,192]{0,1:T(8,128)} async-done(((f32[1152,1536]{0,1:T(8,128)}), f32[1152,192]{0,1:T(8,128)}) %reduce-scatter.29.cloned.1.call-update) | async-done | bytes 884752 | tf_op jit(solution)/shard_map/reduce_scatter | solution.py:217
  1605.9 54.5 %reduce-scatter.33.cloned.1.call-done = f32[64,4]{1,0:T(8,128)} async-done(((f32[512,4]{1,0:T(8,128)}), f32[64,4]{1,0:T(8,128)}) %reduce-scatter.33.cloned.1.call-update) | async-done | bytes 1040
  1661.2 18.6 all-gather.1
  1680.5 45.3 %reduce-scatter.19.cloned.1.call-done = f32[4,16,128]{2,1,0:T(8,128)} async-done(((f32[4,128,128]{2,1,0:T(8,128)}), f32[4,16,128]{2,1,0:T(8,128)}) %reduce-scatter.19.cloned.1.call-update) | async-done | bytes 32784 | tf_op jit(solution)/shard_map/reduce_scatter | solution.py:208
  1726.5 30.6 %all_gather.74 = bf16[4,128,128]{2,1,0:T(8,128)(2,1)S(1)} all-gather(bf16[4,16,128]{2,1,0:T(8,128)(2,1)S(1)} %convert_element_type.250), channel_id=1, replica_groups=mesh['dp'=8,'tensor'=4] {'dp'}, dimensions={1}, use_global_device_ids=true | all-gather | bytes 147456 | tf_op jit(solution)/shard_map/all_gather | solution.py:241
  1757.8 33.4 %reduce-scatter.21.cloned.1.call-done = f32[4,16,128]{2,1,0:T(8,128)} async-done(((f32[4,128,128]{2,1,0:T(8,128)}), f32[4,16,128]{2,1,0:T(8,128)}) %reduce-scatter.21.cloned.1.call-update) | async-done | bytes 32784 | tf_op jit(solution)/shard_map/reduce_scatter | solution.py:210
  1792.0 30.8 %all_gather.76 = bf16[4,128,128]{2,1,0:T(8,128)(2,1)S(1)} all-gather(bf16[4,16,128]{2,1,0:T(8,128)(2,1)S(1)} %convert_element_type.255), channel_id=1, replica_groups=mesh['dp'=8,'tensor'=4] {'dp'}, dimensions={1}, use_global_device_ids=true | all-gather | bytes 147456 | tf_op jit(solution)/shard_map/all_gather | solution.py:247
  1823.5 38.1 %all-reduce.77.cloned.1.call-done = bf16[1024,1536]{1,0:T(8,128)(2,1)} async-done(((bf16[1024,1536]{1,0:T(8,128)(2,1)}), bf16[1024,1536]{1,0:T(8,128)(2,1)}) %all-reduce.77.cloned.1.call-update) | async-done | bytes 3145744 | tf_op jit(solution)/shard_map/psum | solution.py:197
  1861.6 6.8 fusion
  1868.4 38.4 %all-reduce.70 = (bf16[1536]{0:T(1024)(128)(2,1)}, bf16[512]{0:T(512)(128)(2,1)}, bf16[512]{0:T(512)(128)(2,1)}, bf16[512]{0:T(512)(128)(2,1)}, bf16[512]{0:T(51...) all-reduce(f32[1536]{0:T(1024)} %get-tuple-element.116, ...), channel_id=4, replica_groups=mesh['dp'=8,'tensor'=4] {'dp'}, use_global_device_ids=true, to_apply=%region_9.10.clone | all-reduce | flops 6144 | bytes 36864
  1926.3 34.5 %all-reduce.71 = (bf16[1536]{0:T(1024)(128)(2,1)}, bf16[512]{0:T(512)(128)(2,1)}, bf16[512]{0:T(512)(128)(2,1)}, bf16[512]{0:T(512)(128)(2,1)}, bf16[512]{0:T(51...) all-reduce(bf16[1536]{0:T(1024)(128)(2,1)S(1)} %dynamic-update-slic, ...), channel_id=1, replica_groups=mesh['dp'=8,'tensor'=4] {'dp'}, use_global_device_ids=true, to_apply=%add.54 | all-reduce | flops 6144 | bytes 24576
  1984.1 10.3 all-gather.20.cloned.1.call-done
  1997.9 41.1 %all-gather.16.cloned.1.call-done = bf16[1536,512]{1,0:T(8,128)(2,1)} async-done(((bf16[192,512]{1,0:T(8,128)(2,1)}), bf16[1536,512]{1,0:T(8,128)(2,1)}) %all-gather.16.cloned.1.call-update) | async-done | bytes 1572880 | tf_op jit(solution)/shard_map/all_gather | solution.py:223
  2042.6 61.7 %all-gather.22.cloned.1.call-done = bf16[1536,1152]{1,0:T(8,128)(2,1)} async-done(((bf16[192,1152]{1,0:T(8,128)(2,1)}), bf16[1536,1152]{1,0:T(8,128)(2,1)}) %all-gather.22.cloned.1.call-update) | async-done | bytes 3538960 | tf_op jit(solution)/shard_map/all_gather | solution.py:262
  2109.7 60.0 %all-gather.24.cloned.1.call-done = bf16[1536,1152]{1,0:T(8,128)(2,1)} async-done(((bf16[192,1152]{1,0:T(8,128)(2,1)}), bf16[1536,1152]{1,0:T(8,128)(2,1)}) %all-gather.24.cloned.1.call-update) | async-done | bytes 3538960 | tf_op jit(solution)/shard_map/all_gather | solution.py:265
  2175.1 60.1 %all-gather.26.cloned.1.call-done = bf16[1152,1536]{0,1:T(8,128)(2,1)} async-done(((bf16[1152,192]{0,1:T(8,128)(2,1)}), bf16[1152,1536]{0,1:T(8,128)(2,1)}) %all-gather.26.cloned.1.call-update) | async-done | bytes 3538960 | tf_op jit(solution)/shard_map/all_gather | solution.py:268
  2235.2 6.0 copy.116
  (526 shorter events, 563.5 us)
Async XLA Ops:
  7.2 500.6 %copy-start = (bf16[1152,1536]{1,0:T(8,128)(2,1)S(1)}, bf16[1152,1536]{1,0:T(8,128)(2,1)}, u32[]{:S(2)}) copy-start(bf16[1152,1536]{1,0:T(8,128)(2,1)} %param.39) | copy-start | bytes 10616836
  7.2 33.6 %all-gather.12.cloned.1.call-start = ((), (), s32[]{:S(2)}) async-start(), calls=%async_computation.10 | async-start | bytes 3932160 | tf_op jit(solution)/shard_map/all_gather | solution.py:105
  7.9 465.6 %all-gather.28.cloned.1.call-start = ((), (), s32[]{:S(2)}) async-start(), calls=%async_computation.28 | async-start | bytes 31457280 | tf_op jit(solution)/shard_map/all_gather | solution.py:133
  13.9 51.3 %copy-start.15 = (f32[512]{0:T(512)}, f32[512]{0:T(512)S(1)}, u32[]{:S(2)}) copy-start(f32[512]{0:T(512)S(1)} %convert_element_type.215) | copy-start | bytes 6148
  21.2 26.3 %copy-start.17 = (f32[1024]{0:T(1024)}, f32[1024]{0:T(1024)S(1)}, u32[]{:S(2)}) copy-start(f32[1024]{0:T(1024)S(1)} %get-tuple-element.209) | copy-start | bytes 12292
  21.2 26.3 %copy-start.19 = (f32[1024]{0:T(1024)}, f32[1024]{0:T(1024)S(1)}, u32[]{:S(2)}) copy-start(f32[1024]{0:T(1024)S(1)} %get-tuple-element.214) | copy-start | bytes 12292
  21.2 26.3 %copy-start.21 = (f32[1024]{0:T(1024)}, f32[1024]{0:T(1024)S(1)}, u32[]{:S(2)}) copy-start(f32[1024]{0:T(1024)S(1)} %get-tuple-element.215) | copy-start | bytes 12292
  207.7 13.9 copy-start.45
  207.7 13.9 copy-start.59
  234.8 18.4 copy-start.55
  253.2 11.0 copy-start.53
  296.4 8.6 copy-start.24
  296.5 8.6 copy-start.31
  296.5 8.6 copy-start.64
  305.1 9.1 copy-start.74
  318.6 189.1 %all-gather.14.cloned.1.call-start = ((), (), s32[]{:S(2)}) async-start(), calls=%async_computation.11 | async-start | bytes 3932160 | tf_op jit(solution)/shard_map/all_gather | solution.py:148
  319.4 330.9 %all-reduce.75.cloned.1.call-start = ((), (), s32[]{:S(2)}) async-start(), calls=%async_computation.12 | async-start | bytes 12582912 | tf_op jit(solution)/shard_map/psum | solution.py:160
  491.9 4.3 copy-start.70
  496.2 5.8 copy-start.12
  496.2 5.8 copy-start.72
  507.8 12.3 copy-start.71
  520.1 4.3 copy-start.79
  520.1 4.3 copy-start.78
  520.1 4.3 copy-start.73
  530.6 514.8 %reduce-scatter.17.cloned.1.call-start = ((), (), s32[]{:S(2)}) async-start(), calls=%async_computation.16 | async-start | bytes 3538944 | tf_op jit(solution)/shard_map/reduce_scatter | solution.py:204
  650.3 6.4 copy-start.8
  650.3 7.4 copy-start.11
  657.6 4.6 copy-start.77
  661.6 5.8 copy-start.7
  800.6 16.2 copy-start.46
  800.6 16.2 copy-start.60
  830.0 18.4 copy-start.56
  848.4 11.0 copy-start.54
  913.3 16.6 copy-start.16
  913.3 16.6 copy-start.34
  913.3 16.6 copy-start.36
  913.3 16.6 copy-start.48
  929.9 8.4 copy-start.61
  929.9 9.0 copy-start.4
  951.9 6.8 copy-start.2
  951.9 6.8 copy-start.18
  951.9 6.7 copy-start.20
  968.6 151.9 %reduce-scatter.23.cloned.1.call-start = ((), (), s32[]{:S(2)}) async-start(), calls=%async_computation.20 | async-start | bytes 3538944 | tf_op jit(solution)/shard_map/reduce_scatter | solution.py:213
  975.6 222.2 %reduce-scatter.15.cloned.1.call-start = ((), (), s32[]{:S(2)}) async-start(), calls=%async_computation.14 | async-start | bytes 3538944 | tf_op jit(solution)/shard_map/reduce_scatter | solution.py:202
  981.6 348.7 %reduce-scatter.25.cloned.1.call-start = ((), (), s32[]{:S(2)}) async-start(), calls=%async_computation.22 | async-start | bytes 7962624 | tf_op jit(solution)/shard_map/reduce_scatter | solution.py:215
  991.6 471.3 %reduce-scatter.27.cloned.1.call-start = ((), (), s32[]{:S(2)}) async-start(), calls=%async_computation.24 | async-start | bytes 7962624 | tf_op jit(solution)/shard_map/reduce_scatter | solution.py:216
  1001.6 593.6 %reduce-scatter.29.cloned.1.call-start = ((), (), s32[]{:S(2)}) async-start(), calls=%async_computation.26 | async-start | bytes 7962624 | tf_op jit(solution)/shard_map/reduce_scatter | solution.py:217
  1012.0 648.4 %reduce-scatter.33.cloned.1.call-start = ((), (), s32[]{:S(2)}) async-start(), calls=%async_computation.30 | async-start | bytes 294912
  1014.3 711.5 %reduce-scatter.19.cloned.1.call-start = ((), (), s32[]{:S(2)}) async-start(), calls=%async_computation.18 | async-start | bytes 294912 | tf_op jit(solution)/shard_map/reduce_scatter | solution.py:208
  1017.0 774.2 %reduce-scatter.21.cloned.1.call-start = ((), (), s32[]{:S(2)}) async-start(), calls=%async_computation.19 | async-start | bytes 294912 | tf_op jit(solution)/shard_map/reduce_scatter | solution.py:210
  1025.9 835.7 %all-reduce.77.cloned.1.call-start = ((), (), s32[]{:S(2)}) async-start(), calls=%async_computation.13 | async-start | bytes 6291456 | tf_op jit(solution)/shard_map/psum | solution.py:197
  1033.3 942.1 %reduce-scatter.31.cloned.1.call-start = ((), (), s32[]{:S(2)}) async-start(), calls=%async_computation.29 | async-start | bytes 3932160
  1045.3 935.2 %all-gather.18.cloned.1.call-start = ((), (), s32[]{:S(2)}) async-start(), calls=%async_computation.17 | async-start | bytes 1769472 | tf_op jit(solution)/shard_map/all_gather | solution.py:229
  1047.1 947.3 %all-gather.20.cloned.1.call-start = ((), (), s32[]{:S(2)}) async-start(), calls=%async_computation.21 | async-start | bytes 1769472 | tf_op jit(solution)/shard_map/all_gather | solution.py:256
  1122.3 916.8 %all-gather.16.cloned.1.call-start = ((), (), s32[]{:S(2)}) async-start(), calls=%async_computation.15 | async-start | bytes 1769472 | tf_op jit(solution)/shard_map/all_gather | solution.py:223
  1199.5 904.8 %all-gather.22.cloned.1.call-start = ((), (), s32[]{:S(2)}) async-start(), calls=%async_computation.23 | async-start | bytes 3981312 | tf_op jit(solution)/shard_map/all_gather | solution.py:262
  1332.3 265.0 %copy-start.63 = (u32[32]{0:T(128)S(1)}, u32[32]{0:T(128)}, u32[]{:S(2)}) copy-start(u32[32]{0:T(128)} %constant.193) | copy-start | bytes 388
  1332.3 837.3 %all-gather.24.cloned.1.call-start = ((), (), s32[]{:S(2)}) async-start(), calls=%async_computation.25 | async-start | bytes 3981312 | tf_op jit(solution)/shard_map/all_gather | solution.py:265
  1464.8 770.4 %all-gather.26.cloned.1.call-start = ((), (), s32[]{:S(2)}) async-start(), calls=%async_computation.27 | async-start | bytes 3981312 | tf_op jit(solution)/shard_map/all_gather | solution.py:268
  1823.5 44.9 %copy-start.29 = (f32[1536]{0:T(1024)S(1)}, f32[1536]{0:T(1024)}, u32[]{:S(2)}) copy-start(f32[1536]{0:T(1024)} %get-tuple-element.114) | copy-start | bytes 18436
  1823.5 147.4 %copy-start.28 = (f32[1024]{0:T(1024)S(1)}, f32[1024]{0:T(1024)}, u32[]{:S(2)}) copy-start(f32[1024]{0:T(1024)} %copy-done.27) | copy-start | bytes 12292
  1823.5 148.1 %copy-start.26 = (f32[1024]{0:T(1024)S(1)}, f32[1024]{0:T(1024)}, u32[]{:S(2)}) copy-start(f32[1024]{0:T(1024)} %copy-done.23) | copy-start | bytes 12292
  1916.6 5.2 copy-start.68
  1917.5 6.6 copy-start.69
  (37 other events, 93.8 us)
Sparse Core Ops, SparseCore 0:
  9.6 31.1 all-gather.11
  318.8 154.7 all-gather.27
  475.2 28.4 all-gather.13
  530.7 119.5 all-reduce.74
  968.8 74.9 reduce-scatter.16
  1047.2 73.3 reduce-scatter.22
  1124.1 73.5 reduce-scatter.14
  1202.0 128.2 reduce-scatter.24
  1334.5 128.2 reduce-scatter.26
  1466.9 128.2 reduce-scatter.28
  1599.1 61.1 reduce-scatter.32
  1664.1 61.5 reduce-scatter.18
  1729.7 61.5 reduce-scatter.20
  1794.1 67.4 all-reduce.76
  1864.5 37.9 reduce-scatter.30
  1905.2 44.4 all-gather.17
  1951.7 42.7 all-gather.19
  1996.5 42.5 all-gather.15
  2041.3 62.9 all-gather.21
  2106.3 63.3 all-gather.23
  2171.8 63.3 all-gather.25
